TPU v7x, 256 devices: a whole 4x4x8 slice. The times are simulated.
256 devices in a mesh: section: 8 (over y, core), dp: 32 (over x, z).
Axes of the slice: x: 4, y: 4, z: 8, core: 2. Of those that a mesh axis runs over, the one named last changes fastest.
Arguments:
- inputs: bfloat16 [6144, 4096], P('dp'), may hold values from -6 to 6
- output_cotangent: bfloat16 [6144, 4096], P('dp'), may hold values from -6 to 6
- lengths: int32 [64], P('dp'), may hold values from 24 to 96
- query_examples: int32 [16], replicated, may hold values from 0 to 63
- norm_gain: bfloat16 [8, 4096], P('section'), may hold values from 0.5 to 1.5
- value_weight: bfloat16 [8, 4096, 1024], P('section', 'dp'), may hold values from -0.09375 to 0.09375
- output_weight: bfloat16 [8, 4096, 1024], P('section', 'dp'), may hold values from -0.1875 to 0.1875
- input_projection: bfloat16 [8, 32, 4096], P('section'), may hold values from -0.09375 to 0.09375
- output_projection: bfloat16 [8, 32, 1024], P('section'), may hold values from -0.1875 to 0.1875
- fisher_prior: float32 [8, 1024, 1024], P('section'), as said below
Outputs:
- scores: float32 [64, 16], P('dp')
Inputs may be any that keep to these rules, and one draw needn't show every extreme that they name: `fisher_prior`: each block's 1024 x 1024 matrix is symmetric and positive definite.
All inputs are finite; a program needn't handle non-finite values.
Results may differ from a plain program's by a relative error of at most 0.0013.
Values may be sent and summed in bfloat16 or wider, within the bound.
No kernel may reach another device: no remote copies, remote signals or barrier semaphores. Data moves between devices by JAX's collectives and lax.ppermute only.
A program may use at most 128 MiB of HBM per device.

v0:
```python
import jax
import jax.numpy as jnp
from jax import lax
from jax.sharding import PartitionSpec as P


def in_one_piece(arrays, axis, dim, along):
    ends, at = ([], 0)
    for a in arrays[:-1]:
        at += a.shape[along]
        ends.append(at)
    both = jnp.concatenate(arrays, axis=along)
    return tuple(jnp.split(lax.all_gather(both, axis, axis=dim, tiled=True), ends, axis=along))


def shifted(value, axis, steps):
    count = lax.axis_size(axis)
    first, last = (max(0, -steps), min(count, count - steps))
    return lax.ppermute(value, axis, [(source, source + steps) for source in range(first, last)])


def sent_to_all(array, axis):
    size = lax.axis_size(axis)
    return lax.all_to_all(
        jnp.broadcast_to(array[None], (size, *array.shape)), axis, 0, 0, tiled=True
    )


def joined_along(blocks, dim):
    lengths = list(blocks.shape[1:])
    lengths[dim] *= blocks.shape[0]
    return jnp.moveaxis(blocks, 0, dim).reshape(lengths)


def gathered_copies(array, axis, dim):
    blocks = sent_to_all(array, axis)
    return joined_along(blocks, dim)


def taken_together(array, axis):
    return sent_to_all(array, axis).sum(axis=0)


def normalize(hidden, gain):
    widened = hidden.astype(jnp.float32)
    factor = lax.rsqrt(jnp.mean(widened * widened, axis=-1, keepdims=True) + 1e-05)
    return (widened * factor * gain.astype(jnp.float32)).astype(jnp.bfloat16)


def forward_block(hidden, gain, value_map, output_map, input_map):
    normed = normalize(hidden, gain)
    values = jnp.dot(normed, value_map, preferred_element_type=jnp.float32)
    activated = jax.nn.silu(values).astype(jnp.bfloat16)
    branch = lax.dot_general(
        activated, output_map, (((1,), (1,)), ((), ())), preferred_element_type=jnp.float32
    )
    following = (hidden.astype(jnp.float32) + branch).astype(jnp.bfloat16)
    features = lax.dot_general(
        normed, input_map, (((1,), (1,)), ((), ())), preferred_element_type=jnp.float32
    ).astype(jnp.bfloat16)
    return (following, values, features)


def backward_block(hidden, values, cotangent, gain, value_map, output_map, output_map_small):
    widened = hidden.astype(jnp.float32)
    factor = lax.rsqrt(jnp.mean(widened * widened, axis=-1, keepdims=True) + 1e-05)
    upstream = jnp.dot(cotangent, output_map, preferred_element_type=jnp.float32)
    logistic = jax.nn.sigmoid(values)
    slopes = (upstream * logistic * (1.0 + values * (1.0 - logistic))).astype(jnp.bfloat16)
    signals = lax.dot_general(
        slopes, output_map_small, (((1,), (1,)), ((), ())), preferred_element_type=jnp.float32
    ).astype(jnp.bfloat16)
    normed_grad = lax.dot_general(
        slopes, value_map, (((1,), (1,)), ((), ())), preferred_element_type=jnp.float32
    )
    weighted = normed_grad * gain.astype(jnp.float32)
    inner_mean = jnp.mean(weighted * widened, axis=-1, keepdims=True)
    hidden_grad = factor * weighted - widened * (factor * factor * factor) * inner_mean
    previous = (cotangent.astype(jnp.float32) + hidden_grad).astype(jnp.bfloat16)
    return (previous, signals)


def per_device(
    inputs,
    output_cotangent,
    lengths,
    query_examples,
    norm_gain,
    value_weight,
    output_weight,
    input_projection,
    output_projection,
    fisher_prior,
):
    sections = lax.axis_size("section")
    section_index = lax.axis_index("section")
    value_map, output_map = in_one_piece((value_weight, output_weight), "dp", 1, 0)
    value_map = value_map[0]
    output_map = output_map[0]
    gain = norm_gain[0]
    input_map = input_projection[0]
    output_map_small = output_projection[0]
    prior_matrix = fisher_prior[0]
    batches = lengths.shape[0]
    example_rows = inputs.shape[0] // batches
    width = inputs.shape[1]
    value_width = value_map.shape[1]
    feature_width = input_map.shape[0]
    signal_width = output_map_small.shape[0]
    entries = inputs.reshape(batches, example_rows, width)
    positions = jnp.arange(example_rows, dtype=jnp.int32)
    keep = (positions[None, :] < lengths[:, None]).astype(jnp.bfloat16)
    targets = output_cotangent.reshape(batches, example_rows, width) * keep[:, :, None]
    ticks = batches + sections - 1

    def forward_running(hidden):
        return forward_block(hidden, gain, value_map, output_map, input_map)

    def forward_skipped(hidden):
        return (
            jnp.zeros_like(hidden),
            jnp.zeros((example_rows, value_width), jnp.float32),
            jnp.zeros((example_rows, feature_width), jnp.bfloat16),
        )

    def forward_tick(tick, carry):
        incoming, saved_hidden, saved_values, saved_features = carry
        turn = tick - section_index
        active = (turn >= 0) & (turn < batches)
        picked = jnp.clip(turn, 0, batches - 1)
        entering = lax.dynamic_index_in_dim(entries, picked, 0, keepdims=False)
        hidden = jnp.where(section_index == 0, entering, incoming)
        following, values, features = lax.cond(active, forward_running, forward_skipped, hidden)
        saved_hidden = jnp.where(
            active, lax.dynamic_update_index_in_dim(saved_hidden, hidden, picked, 0), saved_hidden
        )
        saved_values = jnp.where(
            active, lax.dynamic_update_index_in_dim(saved_values, values, picked, 0), saved_values
        )
        saved_features = jnp.where(
            active,
            lax.dynamic_update_index_in_dim(saved_features, features, picked, 0),
            saved_features,
        )
        incoming = shifted(following, "section", 1)
        return (incoming, saved_hidden, saved_values, saved_features)

    forward_start = (
        jnp.zeros((example_rows, width), jnp.bfloat16),
        jnp.zeros((batches, example_rows, width), jnp.bfloat16),
        jnp.zeros((batches, example_rows, value_width), jnp.float32),
        jnp.zeros((batches, example_rows, feature_width), jnp.bfloat16),
    )
    forward_state = lax.fori_loop(0, ticks, forward_tick, forward_start)
    saved_hidden = forward_state[1]
    saved_values = forward_state[2]
    saved_features = forward_state[3]

    def backward_running(operands):
        hidden, values, cotangent, features = operands
        previous, signals = backward_block(
            hidden, values, cotangent, gain, value_map, output_map, output_map_small
        )
        grads = (
            lax.dot_general(
                signals, features, (((0,), (0,)), ((), ())), preferred_element_type=jnp.float32
            )
            / example_rows
        )
        return (previous, grads)

    def backward_skipped(operands):
        return (
            jnp.zeros((example_rows, width), jnp.bfloat16),
            jnp.zeros((signal_width, feature_width), jnp.float32),
        )

    def backward_tick(tick, carry):
        incoming, saved_grads = carry
        turn = tick - (sections - 1 - section_index)
        active = (turn >= 0) & (turn < batches)
        picked = jnp.clip(turn, 0, batches - 1)
        arriving = lax.dynamic_index_in_dim(targets, picked, 0, keepdims=False)
        cotangent = jnp.where(section_index == sections - 1, arriving, incoming)
        hidden = lax.dynamic_index_in_dim(saved_hidden, picked, 0, keepdims=False)
        values = lax.dynamic_index_in_dim(saved_values, picked, 0, keepdims=False)
        features = lax.dynamic_index_in_dim(saved_features, picked, 0, keepdims=False)
        previous, grads = lax.cond(
            active, backward_running, backward_skipped, (hidden, values, cotangent, features)
        )
        saved_grads = jnp.where(
            active, lax.dynamic_update_index_in_dim(saved_grads, grads, picked, 0), saved_grads
        )
        incoming = shifted(previous, "section", -1)
        return (incoming, saved_grads)

    backward_start = (
        jnp.zeros((example_rows, width), jnp.bfloat16),
        jnp.zeros((batches, signal_width, feature_width), jnp.float32),
    )
    backward_state = lax.fori_loop(0, ticks, backward_tick, backward_start)
    flat = backward_state[1].reshape(batches, signal_width * feature_width)
    everyone = gathered_copies(flat, "dp", 0)
    fisher = jnp.dot(everyone.T, everyone, precision=lax.Precision.HIGHEST)
    owners = jnp.arange(everyone.shape[0], dtype=jnp.int32)
    selector = (query_examples[:, None] == owners[None, :]).astype(jnp.float32)
    chosen = jnp.dot(selector, everyone, precision=lax.Precision.HIGHEST)
    hessian = prior_matrix + fisher
    lower_factor = jnp.linalg.cholesky(hessian)
    solved = jax.scipy.linalg.cho_solve((lower_factor, True), chosen.T)
    section_scores = jnp.dot(flat, solved, precision=lax.Precision.HIGHEST)
    return taken_together(section_scores, "section")


def solution(mesh):
    placed = (
        P("dp", None),
        P("dp", None),
        P("dp"),
        P(),
        P("section", None),
        P("section", "dp", None),
        P("section", "dp", None),
        P("section", None, None),
        P("section", None, None),
        P("section", None, None),
    )
    return jax.shard_map(
        per_device, mesh=mesh, in_specs=placed, out_specs=P("dp", None), check_vma=False
    )
```

profile of v0, /device:TPU:1, one launch (start us, length us, event | category | flops | bytes accessed | tf_op | source)
XLA Modules:
  0.0 927.9 jit_solution(17330908437757755129)
XLA Ops:
  12.7 141.3 %all-gather.2.cloned.1.call-done = bf16[2,4096,1024]{2,1,0:T(8,128)(2,1)} async-done(((bf16[2,128,1024]{2,1,0:T(8,128)(2,1)}), bf16[2,4096,1024]{2,1,0:T(8,128)(2,1)}) %all-gather.2.cloned.1.call-update) | async-done | bytes 16777232 | tf_op jit(solution)/shard_map/all_gather | solution.py:13
  153.9 11.6 %slice_bitcast_fusion = (bf16[4096,1024]{1,0:T(8,128)(2,1)}, bf16[4096,1024]{1,0:T(8,128)(2,1)}) fusion(bf16[2,4096,1024]{2,1,0:T(8,128)(2,1)} %all-gather.2.cloned.1.call-done), kind=kLoop, calls=%fused_computation.52 | loop fusion | bytes 33554432 | tf_op jit(solution)/shard_map/squeeze | solution.py:99
  165.9 178.0 %while.38 = (s32[]{:T(128)}, bf16[96,4096]{1,0:T(8,128)(2,1)S(1)}, bf16[2,96,4096]{2,1,0:T(8,128)(2,1)S(1)}, f32[2,96,1024]{2,1,0:T(8,128)S(1)}, bf16[2,96,32]{1...) while((s32[]{:T(128)}, bf16[96,4096]{1,0:T(8,128)(2,1)S(1)}, ...), condition=%wide.region_4.5_spmd, body=%wide.region_0.4_spmd.sunk | while | flops 1642670208 | bytes 59466024 | solution.py:154
  169.3 4.0 collective-permute-start
  173.4 9.6 %collective-permute-done = bf16[96,4096]{1,0:T(8,128)(2,1)S(1)} collective-permute-done((bf16[96,4096]{1,0:T(8,128)(2,1)}, bf16[96,4096]{1,0:T(8,128)(2,1)S(1)}, u32[]{:S(2)}, u32[]{:S(2)}) %collective-permute-start) | collective-permute-done | bytes 786464 | tf_op jit(solution)/shard_map/while/body/eval_jaxpr/ppermute | solution.py:19
  184.6 10.3 %conditional.4 = (bf16[96,4096]{1,0:T(8,128)(2,1)S(1)}, f32[1,96,1024]{2,1,0:T(8,128)}, bf16[1,96,32]{1,2,0:T(8,128)(2,1)S(1)}) conditional(s32[]{:T(128)} %convert_element_type.108, () %tuple.154, (bf16[96,4096]{1,0:T(8,128)(2,1)S(1)}, bf16[4096]{0:T(1024)(128)(2,1)S(1)}, bf16[4096,1024]{1,0:T(8,128)(2,1)}, bf16[4096,1024]{1,0:T(8,128)(2,1)}, ...), branch_computations={%region_1.1_spmd, %region_2.3_spmd} | conditional | flops 1641782400 | bytes 48037860 | solution.py:133
  184.9 5.8 fusion.6
  190.8 3.7 fusion
  198.9 8.1 collective-permute-done
  208.6 10.3 %conditional.4 = (bf16[96,4096]{1,0:T(8,128)(2,1)S(1)}, f32[1,96,1024]{2,1,0:T(8,128)}, bf16[1,96,32]{1,2,0:T(8,128)(2,1)S(1)}) conditional(s32[]{:T(128)} %convert_element_type.108, () %tuple.154, (bf16[96,4096]{1,0:T(8,128)(2,1)S(1)}, bf16[4096]{0:T(1024)(128)(2,1)S(1)}, bf16[4096,1024]{1,0:T(8,128)(2,1)}, bf16[4096,1024]{1,0:T(8,128)(2,1)}, ...), branch_computations={%region_1.1_spmd, %region_2.3_spmd} | conditional | flops 1641782400 | bytes 48037860 | solution.py:133
  208.9 5.8 fusion.6
  219.9 4.3 collective-permute-start
  225.2 8.1 collective-permute-done
  236.7 13.8 %collective-permute-start = (bf16[96,4096]{1,0:T(8,128)(2,1)}, bf16[96,4096]{1,0:T(8,128)(2,1)S(1)}, u32[]{:S(2)}, u32[]{:S(2)}) collective-permute-start(bf16[96,4096]{1,0:T(8,128)(2,1)} %copy-done.2), channel_id=1, source_target_pairs={{0,32},{32,64},{64,96},{96,128},{128,160},{160,192},{192,224},{1,3... | collective-permute-start | bytes 2359304 | tf_op jit(solution)/shard_map/while/body/eval_jaxpr/ppermute | solution.py:19
  250.6 9.1 collective-permute-done
  263.0 4.3 collective-permute-start
  267.4 9.1 collective-permute-done
  279.9 4.3 collective-permute-start
  284.3 9.1 collective-permute-done
  296.7 4.3 collective-permute-start
  301.1 9.1 collective-permute-done
  313.6 4.3 collective-permute-start
  318.0 9.1 collective-permute-done
  330.4 4.3 collective-permute-start
  334.8 9.1 collective-permute-done
  344.1 193.4 %while.39 = (s32[]{:T(128)}, bf16[96,4096]{1,0:T(8,128)(2,1)S(1)}, f32[2,32,32]{2,1,0:T(8,128)S(1)}, s32[]{:T(128)}, pred[]{:T(512)}, /*index=5*/bf16[2,96,4096]...) while((s32[]{:T(128)}, bf16[96,4096]{1,0:T(8,128)(2,1)S(1)}, ...), condition=%wide.region_10.11_spmd, body=%wide.region_5.10_spmd.sunk | while | flops 1624286464 | bytes 69592752 | solution.py:201
  347.1 12.2 %collective-permute-done.1 = bf16[96,4096]{1,0:T(8,128)(2,1)S(1)} collective-permute-done((bf16[96,4096]{1,0:T(8,128)(2,1)}, bf16[96,4096]{1,0:T(8,128)(2,1)S(1)}, u32[]{:S(2)}, u32[]{:S(2)}) %collective-permute-start.1) | collective-permute-done | bytes 786464 | tf_op jit(solution)/shard_map/while/body/eval_jaxpr/ppermute | solution.py:19
  362.2 11.6 %collective-permute-done.1 = bf16[96,4096]{1,0:T(8,128)(2,1)S(1)} collective-permute-done((bf16[96,4096]{1,0:T(8,128)(2,1)}, bf16[96,4096]{1,0:T(8,128)(2,1)S(1)}, u32[]{:S(2)}, u32[]{:S(2)}) %collective-permute-start.1) | collective-permute-done | bytes 786464 | tf_op jit(solution)/shard_map/while/body/eval_jaxpr/ppermute | solution.py:19
  376.6 11.6 %collective-permute-done.1 = bf16[96,4096]{1,0:T(8,128)(2,1)S(1)} collective-permute-done((bf16[96,4096]{1,0:T(8,128)(2,1)}, bf16[96,4096]{1,0:T(8,128)(2,1)S(1)}, u32[]{:S(2)}, u32[]{:S(2)}) %collective-permute-start.1) | collective-permute-done | bytes 786464 | tf_op jit(solution)/shard_map/while/body/eval_jaxpr/ppermute | solution.py:19
  391.1 11.6 %collective-permute-done.1 = bf16[96,4096]{1,0:T(8,128)(2,1)S(1)} collective-permute-done((bf16[96,4096]{1,0:T(8,128)(2,1)}, bf16[96,4096]{1,0:T(8,128)(2,1)S(1)}, u32[]{:S(2)}, u32[]{:S(2)}) %collective-permute-start.1) | collective-permute-done | bytes 786464 | tf_op jit(solution)/shard_map/while/body/eval_jaxpr/ppermute | solution.py:19
  405.5 11.6 %collective-permute-done.1 = bf16[96,4096]{1,0:T(8,128)(2,1)S(1)} collective-permute-done((bf16[96,4096]{1,0:T(8,128)(2,1)}, bf16[96,4096]{1,0:T(8,128)(2,1)S(1)}, u32[]{:S(2)}, u32[]{:S(2)}) %collective-permute-start.1) | collective-permute-done | bytes 786464 | tf_op jit(solution)/shard_map/while/body/eval_jaxpr/ppermute | solution.py:19
  420.0 54.9 %collective-permute-done.1 = bf16[96,4096]{1,0:T(8,128)(2,1)S(1)} collective-permute-done((bf16[96,4096]{1,0:T(8,128)(2,1)}, bf16[96,4096]{1,0:T(8,128)(2,1)S(1)}, u32[]{:S(2)}, u32[]{:S(2)}) %collective-permute-start.1) | collective-permute-done | bytes 786464 | tf_op jit(solution)/shard_map/while/body/eval_jaxpr/ppermute | solution.py:19
  474.9 10.5 %conditional.5 = (bf16[96,4096]{1,0:T(8,128)(2,1)}, f32[1,32,32]{2,1,0:T(8,128)S(1)}) conditional(s32[]{:T(128)} %convert_element_type.109, () %tuple.157, (pred[]{:T(512)}, bf16[2,96,4096]{2,1,0:T(8,128)(2,1)}, s32[]{:T(128)}, bf16[96,4096]{1,0:T(8,128)(2,1)S(1)}, bf16[2,96,4096]{2,1,0:T(8,128)(2,1)S(1)}, /*index=5*/bf16[4096,1024]{1,0:T(8,128)(2,1)}, ...), branch_computations={%region_6.6_spmd, %region_7.9_spmd} | conditional | flops 1624285440 | bytes 66397524 | solution.py:188
  474.9 5.2 fusion.18
  487.4 11.6 %collective-permute-done.1 = bf16[96,4096]{1,0:T(8,128)(2,1)S(1)} collective-permute-done((bf16[96,4096]{1,0:T(8,128)(2,1)}, bf16[96,4096]{1,0:T(8,128)(2,1)S(1)}, u32[]{:S(2)}, u32[]{:S(2)}) %collective-permute-start.1) | collective-permute-done | bytes 786464 | tf_op jit(solution)/shard_map/while/body/eval_jaxpr/ppermute | solution.py:19
  499.0 10.5 %conditional.5 = (bf16[96,4096]{1,0:T(8,128)(2,1)}, f32[1,32,32]{2,1,0:T(8,128)S(1)}) conditional(s32[]{:T(128)} %convert_element_type.109, () %tuple.157, (pred[]{:T(512)}, bf16[2,96,4096]{2,1,0:T(8,128)(2,1)}, s32[]{:T(128)}, bf16[96,4096]{1,0:T(8,128)(2,1)S(1)}, bf16[2,96,4096]{2,1,0:T(8,128)(2,1)S(1)}, /*index=5*/bf16[4096,1024]{1,0:T(8,128)(2,1)}, ...), branch_computations={%region_6.6_spmd, %region_7.9_spmd} | conditional | flops 1624285440 | bytes 66397524 | solution.py:188
  499.0 5.2 fusion.18
  511.5 11.6 %collective-permute-done.1 = bf16[96,4096]{1,0:T(8,128)(2,1)S(1)} collective-permute-done((bf16[96,4096]{1,0:T(8,128)(2,1)}, bf16[96,4096]{1,0:T(8,128)(2,1)S(1)}, u32[]{:S(2)}, u32[]{:S(2)}) %collective-permute-start.1) | collective-permute-done | bytes 786464 | tf_op jit(solution)/shard_map/while/body/eval_jaxpr/ppermute | solution.py:19
  526.4 11.1 %collective-permute-done.1 = bf16[96,4096]{1,0:T(8,128)(2,1)S(1)} collective-permute-done((bf16[96,4096]{1,0:T(8,128)(2,1)}, bf16[96,4096]{1,0:T(8,128)(2,1)S(1)}, u32[]{:S(2)}, u32[]{:S(2)}) %collective-permute-start.1) | collective-permute-done | bytes 786464 | tf_op jit(solution)/shard_map/while/body/eval_jaxpr/ppermute | solution.py:19
  538.4 15.8 %all-to-all-start = ((f32[32,2,1024]{2,1,0:T(2,128)}), f32[32,2,1024]{2,1,0:T(2,128)S(1)}, u32[]{:S(2)}, u32[]{:S(2)}) async-start(f32[32,2,1024]{2,1,0:T(2,128)} %broadcast_in_dim.89), calls=%async_computation | async-start | bytes 524288 | tf_op jit(solution)/shard_map/all_to_all | solution.py:24
  554.2 5.4 copy.33
  559.5 4.0 all-to-all-done
  563.5 6.6 bitcast_add_fusion.1
  570.1 5.3 copy.37
  575.4 4.4 fusion.28
  581.8 11.7 %cholesky.223 = f32[128,128]{1,0:T(8,128)S(1)} custom-call(f32[128,128]{1,0:T(8,128)S(1)} %cholesky.580), custom_call_target="Cholesky" | custom-call | tf_op jit(solution)/shard_map/jit(cholesky)/cholesky | solution.py:209
  596.0 9.8 %custom-call.66 = f32[1,128,128]{1,2,0:T(8,128)S(1)} custom-call(f32[1,128,128]{2,1,0:T(8,128)S(1)} %get-tuple-element.814), custom_call_target="InvertDiagBlocksLowerTriangular" | custom-call | tf_op jit(solution)/shard_map/jit(cholesky)/cholesky | solution.py:209
  609.8 12.1 %cholesky.244 = f32[128,128]{1,0:T(8,128)S(1)} custom-call(f32[128,128]{1,0:T(8,128)S(1)} %cholesky.584), custom_call_target="Cholesky" | custom-call | tf_op jit(solution)/shard_map/jit(cholesky)/cholesky | solution.py:209
  622.5 9.8 %custom-call.67 = f32[1,128,128]{1,2,0:T(8,128)S(1)} custom-call(f32[1,128,128]{2,1,0:T(8,128)S(1)} %get-tuple-element.811), custom_call_target="InvertDiagBlocksLowerTriangular" | custom-call | tf_op jit(solution)/shard_map/jit(cholesky)/cholesky | solution.py:209
  635.7 11.7 %cholesky.468 = f32[128,128]{1,0:T(8,128)S(1)} custom-call(f32[128,128]{1,0:T(8,128)S(1)} %cholesky.589), custom_call_target="Cholesky" | custom-call | tf_op jit(solution)/shard_map/jit(cholesky)/cholesky | solution.py:209
  648.7 9.8 %custom-call.68 = f32[1,128,128]{1,2,0:T(8,128)S(1)} custom-call(f32[1,128,128]{2,1,0:T(8,128)S(1)} %get-tuple-element.808), custom_call_target="InvertDiagBlocksLowerTriangular" | custom-call | tf_op jit(solution)/shard_map/jit(cholesky)/cholesky | solution.py:209
  662.0 11.8 %cholesky.487 = f32[128,128]{1,0:T(8,128)S(1)} custom-call(f32[128,128]{1,0:T(8,128)S(1)} %cholesky.594), custom_call_target="Cholesky" | custom-call | tf_op jit(solution)/shard_map/jit(cholesky)/cholesky | solution.py:209
  675.1 9.8 %custom-call.69 = f32[1,128,128]{1,2,0:T(8,128)S(1)} custom-call(f32[1,128,128]{2,1,0:T(8,128)S(1)} %get-tuple-element.805), custom_call_target="InvertDiagBlocksLowerTriangular" | custom-call | tf_op jit(solution)/shard_map/jit(cholesky)/cholesky | solution.py:209
  688.4 11.7 %cholesky.506 = f32[128,128]{1,0:T(8,128)S(1)} custom-call(f32[128,128]{1,0:T(8,128)S(1)} %cholesky.599), custom_call_target="Cholesky" | custom-call | tf_op jit(solution)/shard_map/jit(cholesky)/cholesky | solution.py:209
  701.4 10.0 %custom-call.70 = f32[1,128,128]{1,2,0:T(8,128)S(1)} custom-call(f32[1,128,128]{2,1,0:T(8,128)S(1)} %get-tuple-element.802), custom_call_target="InvertDiagBlocksLowerTriangular" | custom-call | tf_op jit(solution)/shard_map/jit(cholesky)/cholesky | solution.py:209
  714.7 11.7 %cholesky.526 = f32[128,128]{1,0:T(8,128)S(1)} custom-call(f32[128,128]{1,0:T(8,128)S(1)} %cholesky.604), custom_call_target="Cholesky" | custom-call | tf_op jit(solution)/shard_map/jit(cholesky)/cholesky | solution.py:209
  727.7 9.8 %custom-call.71 = f32[1,128,128]{1,2,0:T(8,128)S(1)} custom-call(f32[1,128,128]{2,1,0:T(8,128)S(1)} %get-tuple-element.799), custom_call_target="InvertDiagBlocksLowerTriangular" | custom-call | tf_op jit(solution)/shard_map/jit(cholesky)/cholesky | solution.py:209
  740.5 12.1 %cholesky.546 = f32[128,128]{1,0:T(8,128)S(1)} custom-call(f32[128,128]{1,0:T(8,128)S(1)} %cholesky.609), custom_call_target="Cholesky" | custom-call | tf_op jit(solution)/shard_map/jit(cholesky)/cholesky | solution.py:209
  753.9 9.8 %custom-call.72 = f32[1,128,128]{1,2,0:T(8,128)S(1)} custom-call(f32[1,128,128]{2,1,0:T(8,128)S(1)} %get-tuple-element.796), custom_call_target="InvertDiagBlocksLowerTriangular" | custom-call | tf_op jit(solution)/shard_map/jit(cholesky)/cholesky | solution.py:209
  766.3 11.7 %cholesky.564 = f32[128,128]{1,0:T(8,128)S(1)} custom-call(f32[128,128]{1,0:T(8,128)S(1)} %convolution_subtract_fusion.6), custom_call_target="Cholesky" | custom-call | tf_op jit(solution)/shard_map/jit(cholesky)/cholesky | solution.py:209
  784.9 4.8 select_select_fusion
  789.7 22.8 %while.40 = (s32[]{:T(128)}, f32[1024,1024]{1,0:T(8,128)}, s32[8,2]{0,1:T(2,128)S(1)}, f32[8,128,128]{2,1,0:T(8,128)S(1)}, s32[]{:T(128)}) while((s32[]{:T(128)}, f32[1024,1024]{1,0:T(8,128)}, s32[8,2]{0,1:T(2,128)S(1)}, f32[8,128,128]{2,1,0:T(8,128)S(1)}, s32[]{:T(128)}) %tuple.171), condition=%wide.while_cond, body=%wide.while_body.sunk | while | flops 2 | bytes 131181 | solution.py:210
  812.5 78.8 %custom-call.73 = f32[8,128,128]{1,2,0:T(8,128)S(1)} custom-call(f32[8,128,128]{2,1,0:T(8,128)S(1)} %get-tuple-element.657), custom_call_target="InvertDiagBlocksLowerTriangular" | custom-call | tf_op jit(solution)/shard_map/jit(_cho_solve)/triangular_solve | solution.py:210
  912.8 7.5 all_to_all.10
  (296 shorter events, 174.6 us)
Async XLA Ops:
  6.5 147.4 %all-gather.2.cloned.1.call-start = ((), (), s32[]{:S(2)}) async-start(), calls=%async_computation.2 | async-start | bytes 17301504 | tf_op jit(solution)/shard_map/all_gather | solution.py:13
  165.9 178.2 %copy-start.4 = (bf16[1,32,1024]{2,1,0:T(8,128)(2,1)S(1)}, bf16[1,32,1024]{2,1,0:T(8,128)(2,1)}, u32[]{:S(2)}) copy-start(bf16[1,32,1024]{2,1,0:T(8,128)(2,1)} %param.26) | copy-start | bytes 196612
  168.4 0.9 copy-start.2
  169.3 13.8 %collective-permute-start = (bf16[96,4096]{1,0:T(8,128)(2,1)}, bf16[96,4096]{1,0:T(8,128)(2,1)S(1)}, u32[]{:S(2)}, u32[]{:S(2)}) collective-permute-start(bf16[96,4096]{1,0:T(8,128)(2,1)} %copy-done.2), channel_id=1, source_target_pairs={{0,32},{32,64},{64,96},{96,128},{128,160},{160,192},{192,224},{1,3... | collective-permute-start | bytes 2359304 | tf_op jit(solution)/shard_map/while/body/eval_jaxpr/ppermute | solution.py:19
  184.7 6.1 slice-start
  184.9 5.8 slice-start.1
  190.8 3.8 copy-start.6
  195.0 0.9 copy-start.2
  195.9 11.1 %collective-permute-start = (bf16[96,4096]{1,0:T(8,128)(2,1)}, bf16[96,4096]{1,0:T(8,128)(2,1)S(1)}, u32[]{:S(2)}, u32[]{:S(2)}) collective-permute-start(bf16[96,4096]{1,0:T(8,128)(2,1)} %copy-done.2), channel_id=1, source_target_pairs={{0,32},{32,64},{64,96},{96,128},{128,160},{160,192},{192,224},{1,3... | collective-permute-start | bytes 2359304 | tf_op jit(solution)/shard_map/while/body/eval_jaxpr/ppermute | solution.py:19
  208.6 6.1 slice-start
  208.9 5.8 slice-start.1
  214.7 3.8 copy-start.6
  219.0 0.9 copy-start.2
  219.9 13.5 %collective-permute-start = (bf16[96,4096]{1,0:T(8,128)(2,1)}, bf16[96,4096]{1,0:T(8,128)(2,1)S(1)}, u32[]{:S(2)}, u32[]{:S(2)}) collective-permute-start(bf16[96,4096]{1,0:T(8,128)(2,1)} %copy-done.2), channel_id=1, source_target_pairs={{0,32},{32,64},{64,96},{96,128},{128,160},{160,192},{192,224},{1,3... | collective-permute-start | bytes 2359304 | tf_op jit(solution)/shard_map/while/body/eval_jaxpr/ppermute | solution.py:19
  235.8 0.9 copy-start.2
  236.7 23.0 %collective-permute-start = (bf16[96,4096]{1,0:T(8,128)(2,1)}, bf16[96,4096]{1,0:T(8,128)(2,1)S(1)}, u32[]{:S(2)}, u32[]{:S(2)}) collective-permute-start(bf16[96,4096]{1,0:T(8,128)(2,1)} %copy-done.2), channel_id=1, source_target_pairs={{0,32},{32,64},{64,96},{96,128},{128,160},{160,192},{192,224},{1,3... | collective-permute-start | bytes 2359304 | tf_op jit(solution)/shard_map/while/body/eval_jaxpr/ppermute | solution.py:19
  262.2 0.9 copy-start.2
  263.0 13.5 %collective-permute-start = (bf16[96,4096]{1,0:T(8,128)(2,1)}, bf16[96,4096]{1,0:T(8,128)(2,1)S(1)}, u32[]{:S(2)}, u32[]{:S(2)}) collective-permute-start(bf16[96,4096]{1,0:T(8,128)(2,1)} %copy-done.2), channel_id=1, source_target_pairs={{0,32},{32,64},{64,96},{96,128},{128,160},{160,192},{192,224},{1,3... | collective-permute-start | bytes 2359304 | tf_op jit(solution)/shard_map/while/body/eval_jaxpr/ppermute | solution.py:19
  279.0 0.9 copy-start.2
  279.9 13.5 %collective-permute-start = (bf16[96,4096]{1,0:T(8,128)(2,1)}, bf16[96,4096]{1,0:T(8,128)(2,1)S(1)}, u32[]{:S(2)}, u32[]{:S(2)}) collective-permute-start(bf16[96,4096]{1,0:T(8,128)(2,1)} %copy-done.2), channel_id=1, source_target_pairs={{0,32},{32,64},{64,96},{96,128},{128,160},{160,192},{192,224},{1,3... | collective-permute-start | bytes 2359304 | tf_op jit(solution)/shard_map/while/body/eval_jaxpr/ppermute | solution.py:19
  295.9 0.9 copy-start.2
  296.7 13.5 %collective-permute-start = (bf16[96,4096]{1,0:T(8,128)(2,1)}, bf16[96,4096]{1,0:T(8,128)(2,1)S(1)}, u32[]{:S(2)}, u32[]{:S(2)}) collective-permute-start(bf16[96,4096]{1,0:T(8,128)(2,1)} %copy-done.2), channel_id=1, source_target_pairs={{0,32},{32,64},{64,96},{96,128},{128,160},{160,192},{192,224},{1,3... | collective-permute-start | bytes 2359304 | tf_op jit(solution)/shard_map/while/body/eval_jaxpr/ppermute | solution.py:19
  312.7 0.9 copy-start.2
  313.6 13.5 %collective-permute-start = (bf16[96,4096]{1,0:T(8,128)(2,1)}, bf16[96,4096]{1,0:T(8,128)(2,1)S(1)}, u32[]{:S(2)}, u32[]{:S(2)}) collective-permute-start(bf16[96,4096]{1,0:T(8,128)(2,1)} %copy-done.2), channel_id=1, source_target_pairs={{0,32},{32,64},{64,96},{96,128},{128,160},{160,192},{192,224},{1,3... | collective-permute-start | bytes 2359304 | tf_op jit(solution)/shard_map/while/body/eval_jaxpr/ppermute | solution.py:19
  329.5 0.9 copy-start.2
  330.4 13.5 %collective-permute-start = (bf16[96,4096]{1,0:T(8,128)(2,1)}, bf16[96,4096]{1,0:T(8,128)(2,1)S(1)}, u32[]{:S(2)}, u32[]{:S(2)}) collective-permute-start(bf16[96,4096]{1,0:T(8,128)(2,1)} %copy-done.2), channel_id=1, source_target_pairs={{0,32},{32,64},{64,96},{96,128},{128,160},{160,192},{192,224},{1,3... | collective-permute-start | bytes 2359304 | tf_op jit(solution)/shard_map/while/body/eval_jaxpr/ppermute | solution.py:19
  345.1 14.1 %collective-permute-start.1 = (bf16[96,4096]{1,0:T(8,128)(2,1)}, bf16[96,4096]{1,0:T(8,128)(2,1)S(1)}, u32[]{:S(2)}, u32[]{:S(2)}) collective-permute-start(bf16[96,4096]{1,0:T(8,128)(2,1)} %get-tuple-element.1037), channel_id=1, source_target_pairs={{32,0},{64,32},{96,64},{128,96},{160,128},{192,160},{224,192},{33,... | collective-permute-start | bytes 2359304 | tf_op jit(solution)/shard_map/while/body/eval_jaxpr/ppermute | solution.py:19
  360.2 13.5 %collective-permute-start.1 = (bf16[96,4096]{1,0:T(8,128)(2,1)}, bf16[96,4096]{1,0:T(8,128)(2,1)S(1)}, u32[]{:S(2)}, u32[]{:S(2)}) collective-permute-start(bf16[96,4096]{1,0:T(8,128)(2,1)} %get-tuple-element.1037), channel_id=1, source_target_pairs={{32,0},{64,32},{96,64},{128,96},{160,128},{192,160},{224,192},{33,... | collective-permute-start | bytes 2359304 | tf_op jit(solution)/shard_map/while/body/eval_jaxpr/ppermute | solution.py:19
  374.7 13.5 %collective-permute-start.1 = (bf16[96,4096]{1,0:T(8,128)(2,1)}, bf16[96,4096]{1,0:T(8,128)(2,1)S(1)}, u32[]{:S(2)}, u32[]{:S(2)}) collective-permute-start(bf16[96,4096]{1,0:T(8,128)(2,1)} %get-tuple-element.1037), channel_id=1, source_target_pairs={{32,0},{64,32},{96,64},{128,96},{160,128},{192,160},{224,192},{33,... | collective-permute-start | bytes 2359304 | tf_op jit(solution)/shard_map/while/body/eval_jaxpr/ppermute | solution.py:19
  389.1 13.5 %collective-permute-start.1 = (bf16[96,4096]{1,0:T(8,128)(2,1)}, bf16[96,4096]{1,0:T(8,128)(2,1)S(1)}, u32[]{:S(2)}, u32[]{:S(2)}) collective-permute-start(bf16[96,4096]{1,0:T(8,128)(2,1)} %get-tuple-element.1037), channel_id=1, source_target_pairs={{32,0},{64,32},{96,64},{128,96},{160,128},{192,160},{224,192},{33,... | collective-permute-start | bytes 2359304 | tf_op jit(solution)/shard_map/while/body/eval_jaxpr/ppermute | solution.py:19
  403.6 13.5 %collective-permute-start.1 = (bf16[96,4096]{1,0:T(8,128)(2,1)}, bf16[96,4096]{1,0:T(8,128)(2,1)S(1)}, u32[]{:S(2)}, u32[]{:S(2)}) collective-permute-start(bf16[96,4096]{1,0:T(8,128)(2,1)} %get-tuple-element.1037), channel_id=1, source_target_pairs={{32,0},{64,32},{96,64},{128,96},{160,128},{192,160},{224,192},{33,... | collective-permute-start | bytes 2359304 | tf_op jit(solution)/shard_map/while/body/eval_jaxpr/ppermute | solution.py:19
  418.1 56.9 %collective-permute-start.1 = (bf16[96,4096]{1,0:T(8,128)(2,1)}, bf16[96,4096]{1,0:T(8,128)(2,1)S(1)}, u32[]{:S(2)}, u32[]{:S(2)}) collective-permute-start(bf16[96,4096]{1,0:T(8,128)(2,1)} %get-tuple-element.1037), channel_id=1, source_target_pairs={{32,0},{64,32},{96,64},{128,96},{160,128},{192,160},{224,192},{33,... | collective-permute-start | bytes 2359304 | tf_op jit(solution)/shard_map/while/body/eval_jaxpr/ppermute | solution.py:19
  474.9 6.0 copy-start
  480.9 2.8 copy-start.1
  485.5 13.5 %collective-permute-start.1 = (bf16[96,4096]{1,0:T(8,128)(2,1)}, bf16[96,4096]{1,0:T(8,128)(2,1)S(1)}, u32[]{:S(2)}, u32[]{:S(2)}) collective-permute-start(bf16[96,4096]{1,0:T(8,128)(2,1)} %get-tuple-element.1037), channel_id=1, source_target_pairs={{32,0},{64,32},{96,64},{128,96},{160,128},{192,160},{224,192},{33,... | collective-permute-start | bytes 2359304 | tf_op jit(solution)/shard_map/while/body/eval_jaxpr/ppermute | solution.py:19
  499.0 6.0 copy-start
  505.0 2.8 copy-start.1
  509.5 13.5 %collective-permute-start.1 = (bf16[96,4096]{1,0:T(8,128)(2,1)}, bf16[96,4096]{1,0:T(8,128)(2,1)S(1)}, u32[]{:S(2)}, u32[]{:S(2)}) collective-permute-start(bf16[96,4096]{1,0:T(8,128)(2,1)} %get-tuple-element.1037), channel_id=1, source_target_pairs={{32,0},{64,32},{96,64},{128,96},{160,128},{192,160},{224,192},{33,... | collective-permute-start | bytes 2359304 | tf_op jit(solution)/shard_map/while/body/eval_jaxpr/ppermute | solution.py:19
  524.0 13.5 %collective-permute-start.1 = (bf16[96,4096]{1,0:T(8,128)(2,1)}, bf16[96,4096]{1,0:T(8,128)(2,1)S(1)}, u32[]{:S(2)}, u32[]{:S(2)}) collective-permute-start(bf16[96,4096]{1,0:T(8,128)(2,1)} %get-tuple-element.1037), channel_id=1, source_target_pairs={{32,0},{64,32},{96,64},{128,96},{160,128},{192,160},{224,192},{33,... | collective-permute-start | bytes 2359304 | tf_op jit(solution)/shard_map/while/body/eval_jaxpr/ppermute | solution.py:19
  538.4 25.1 %all-to-all-start = ((f32[32,2,1024]{2,1,0:T(2,128)}), f32[32,2,1024]{2,1,0:T(2,128)S(1)}, u32[]{:S(2)}, u32[]{:S(2)}) async-start(f32[32,2,1024]{2,1,0:T(2,128)} %broadcast_in_dim.89), calls=%async_computation | async-start | bytes 524288 | tf_op jit(solution)/shard_map/all_to_all | solution.py:24
  579.9 1.9 copy-start.3
  784.8 106.6 %copy-start.5 = (s32[16]{0:T(128)S(1)}, s32[16]{0:T(128)}, u32[]{:S(2)}) copy-start(s32[16]{0:T(128)} %param.21) | copy-start | bytes 196
Sparse Core Ops, SparseCore 0:
  9.9 143.9 all-gather.1
where the time goes:
time: 938 us; the launch traced here: 928 us
  waiting for transfers between devices  374 us (40%)
  other arithmetic  288 us (31%)
  matrix products  87.2 us (9%)
  starting transfers between devices  78.8 us (8%)
  local copies, waits for them, and re-layouts  73.4 us (8%)
  between operations  18.9 us (2%)
    ppermute x18, waiting for transfers between devices, shifted(): lax.ppermute(value, axis, [(source, source + steps) for source in range(f...  228 us
    another operation x30, other arithmetic, per_device(): lower_factor = jnp.linalg.cholesky(hessian)  172 us
    all_gather x1, waiting for transfers between devices, in_one_piece(): lax.all_gather(both, axis, axis=dim, tiled=True)  141 us
    another operation x3, other arithmetic, per_device(): solved = jax.scipy.linalg.cho_solve((lower_factor, True), chosen.T)  83.6 us
    ppermute x18, starting transfers between devices, shifted(): lax.ppermute(value, axis, [(source, source + steps) for source in range(f...  63 us
    another operation x40, local copies, waits for them, and re-layouts  29.9 us
    another operation x14, matrix products, per_device(): lower_factor = jnp.linalg.cholesky(hessian)  23.1 us
    another operation x30, matrix products, per_device(): solved = jax.scipy.linalg.cho_solve((lower_factor, True), chosen.T)  20.6 us
  transfers between devices with their start and end apart: 20, of which 20 were waited for; matrix products, arithmetic and copies ran while one was open for 1% of the time, Pallas kernels for 0%

commit v1 on v0

v1 whole, which is shorter than its diff:
```python
import jax
import jax.numpy as jnp
from jax import lax
from jax.experimental import pallas as pl
from jax.experimental.pallas import tpu as pltpu
from jax.sharding import PartitionSpec as P

EXACT = lax.Precision.HIGHEST
BLOCK = 128
CHUNK = 512
f32 = jnp.float32
bf16 = jnp.bfloat16
NT = (((1,), (1,)), ((), ()))
TN = (((0,), (0,)), ((), ()))
MEBI = 1 << 20


def whole():
    return pl.BlockSpec(memory_space=pltpu.VMEM)


def swept(block):
    size = block.shape[0]
    lanes = lax.broadcasted_iota(jnp.int32, (1, size), 1)
    rows = lax.broadcasted_iota(jnp.int32, (size, 1), 0)
    for at in range(size):
        column = block[:, at : at + 1]
        row = block[at : at + 1, :]
        inverse = 1.0 / column[at : at + 1, :]
        scaled = jnp.where(lanes == at, -inverse, row * inverse)
        column = jnp.where(rows == at, -1.0, column)
        kept = jnp.where((lanes == at) | (rows == at), 0.0, block)
        block = kept - column * scaled
    return block


def exact_dot(a, b):
    return jnp.dot(a, b, precision=EXACT, preferred_element_type=f32)


def inverse_kernel(prior, out):
    size = prior.shape[0]
    tall = min(256, size)
    out[...] = prior[...]

    def step(turn, _):
        span = pl.ds(pl.multiple_of(turn * BLOCK, BLOCK), BLOCK)
        pivot = swept(out[span, span])
        left = out[:, span]
        above = out[span, :]
        right = -exact_dot(left, pivot)
        below = -exact_dot(pivot, above)
        for row in range(0, size, tall):
            out[row : row + tall, :] -= exact_dot(right[row : row + tall], above)
        out[:, span] = right
        out[span, :] = below
        out[span, span] = pivot
        return 0

    lax.fori_loop(0, size // BLOCK, step, 0)


def minus_inverse(prior):
    size = prior.shape[0]
    return pl.pallas_call(
        inverse_kernel,
        out_shape=jax.ShapeDtypeStruct(prior.shape, f32),
        in_specs=[whole()],
        out_specs=whole(),
        compiler_params=pltpu.CompilerParams(vmem_limit_bytes=32 * MEBI),
        cost_estimate=pl.CostEstimate(
            flops=60 * size**3, bytes_accessed=8 * size * size, transcendentals=0
        ),
        name="prior_inverse",
    )(prior)


def inverse_root(hidden):
    return lax.rsqrt(jnp.mean(hidden * hidden, axis=-1, keepdims=True) + 1e-05)


def forward_kernel(
    flags, entry, incoming, gain, weights, input_map, kept_hidden, kept_values, kept_features,
    following, hidden_out, values_out, features_out, normed, activated,
):
    active, first, last = (flags[0], flags[1], flags[2])
    width = incoming.shape[1]

    @pl.when(active == 1)
    def _():
        hidden = jnp.where(first == 1, entry[0], incoming[...])
        hidden_out[0] = hidden
        widened = hidden.astype(f32)
        normed[...] = (widened * inverse_root(widened) * gain[...].astype(f32)).astype(bf16)
        values = jnp.dot(normed[...], weights[0], preferred_element_type=f32)
        values_out[0] = values
        activated[...] = (values * jax.nn.sigmoid(values)).astype(bf16)

        @pl.when(last == 0)
        def _():
            for at in range(0, width, CHUNK):
                branch = lax.dot_general(
                    activated[...], weights[1, at : at + CHUNK, :], NT, preferred_element_type=f32
                )
                kept = hidden_out[0, :, at : at + CHUNK].astype(f32)
                following[:, at : at + CHUNK] = (kept + branch).astype(bf16)

        features_out[0] = lax.dot_general(
            normed[...], input_map[...], NT, preferred_element_type=f32
        ).astype(bf16)


def backward_kernel(
    flags, entry, incoming, kept_hidden, kept_values, kept_features, gain, weights, output_map,
    kept_grads, previous, grads_out, weighted, slopes,
):
    active, first, last = (flags[0], flags[1], flags[2])
    rows, width = incoming.shape

    @pl.when(active == 1)
    def _():
        cotangent = jnp.where(last == 1, entry[0], incoming[...])
        upstream = jnp.dot(cotangent, weights[1], preferred_element_type=f32)
        values = kept_values[0]
        logistic = jax.nn.sigmoid(values)
        slopes[...] = (upstream * logistic * (1.0 + values * (1.0 - logistic))).astype(bf16)

        @pl.when(first == 0)
        def _():
            widened = kept_hidden[0].astype(f32)
            factor = inverse_root(widened)
            inner = jnp.zeros((rows, 1), f32)
            for at in range(0, width, CHUNK):
                part = lax.dot_general(
                    slopes[...], weights[0, at : at + CHUNK, :], NT, preferred_element_type=f32
                ) * gain[:, at : at + CHUNK].astype(f32)
                weighted[:, at : at + CHUNK] = part
                inner += jnp.sum(
                    part * kept_hidden[0, :, at : at + CHUNK].astype(f32), axis=-1, keepdims=True
                )
            pull = (factor * factor * factor) * (inner / width)
            for at in range(0, width, CHUNK):
                span = slice(at, at + CHUNK)
                arrived = jnp.where(last == 1, entry[0, :, span], incoming[:, span]).astype(f32)
                hidden_grad = factor * weighted[:, span] - kept_hidden[0, :, span].astype(f32) * pull
                previous[:, span] = (arrived + hidden_grad).astype(bf16)

        signals = lax.dot_general(
            slopes[...], output_map[...], NT, preferred_element_type=f32
        ).astype(bf16)
        grads_out[0] = (
            lax.dot_general(signals, kept_features[0], TN, preferred_element_type=f32) / rows
        )


def scores_kernel(every, own, inverse, select, out):
    count = every.shape[0]
    queries = select.shape[1]
    against = exact_dot(every[...], inverse[...])
    gram = -lax.dot_general(
        against, every[...], NT, precision=EXACT, preferred_element_type=f32
    )
    eye = (
        lax.broadcasted_iota(jnp.int32, (count, count), 0)
        == lax.broadcasted_iota(jnp.int32, (count, count), 1)
    ).astype(f32)
    solved = -exact_dot(swept(gram + eye), exact_dot(gram, select[...]))
    out[...] = exact_dot(own[...], solved)


def per_device(
    inputs,
    output_cotangent,
    lengths,
    query_examples,
    norm_gain,
    value_weight,
    output_weight,
    input_projection,
    output_projection,
    fisher_prior,
):
    sections = lax.axis_size("section")
    section = lax.axis_index("section")
    both = jnp.concatenate([value_weight, output_weight], axis=0)
    weights = lax.all_gather(both, "dp", axis=1, tiled=True)
    inverse = minus_inverse(fisher_prior[0])
    weights = pltpu.with_memory_space_constraint(weights, pltpu.VMEM)
    input_map = input_projection[0]
    output_map = output_projection[0]
    batches = lengths.shape[0]
    rows = inputs.shape[0] // batches
    width = inputs.shape[1]
    inner = weights.shape[2]
    features = input_map.shape[0]
    signals = output_map.shape[0]
    entries = inputs.reshape(batches, rows, width)
    positions = jnp.arange(rows, dtype=jnp.int32)
    keep = (positions[None, :] < lengths[:, None]).astype(bf16)
    targets = output_cotangent.reshape(batches, rows, width) * keep[:, :, None]
    first = (section == 0).astype(jnp.int32)
    last = (section == sections - 1).astype(jnp.int32)

    def flags_at(turn):
        active = (turn >= 0) & (turn < batches)
        entry = jnp.clip(turn, 0, batches - 1)
        slot = jnp.where(active, turn, batches)
        return jnp.stack([active.astype(jnp.int32), first, last, slot, entry]).astype(jnp.int32)

    def slotted(shape):
        return pl.BlockSpec((1, *shape), lambda _, flags: (flags[3], 0, 0))

    def entering():
        return pl.BlockSpec((1, rows, width), lambda _, flags: (flags[4], 0, 0))

    untouched = pl.BlockSpec(memory_space=pl.ANY)
    flops = 4 * rows * width * inner
    cost = pl.CostEstimate(flops=flops, bytes_accessed=4 * width * inner, transcendentals=0)

    def forward(flags, incoming, state):
        shapes = ((rows, width), (rows, inner), (rows, features))
        following, *state = pl.pallas_call(
            forward_kernel,
            grid_spec=pltpu.PrefetchScalarGridSpec(
                num_scalar_prefetch=1,
                grid=(1,),
                in_specs=[entering(), whole(), whole(), whole(), whole()] + [untouched] * 3,
                out_specs=[whole()] + [slotted(shape) for shape in shapes],
                scratch_shapes=[pltpu.VMEM((rows, width), bf16), pltpu.VMEM((rows, inner), bf16)],
            ),
            out_shape=[jax.ShapeDtypeStruct((rows, width), bf16)]
            + [jax.ShapeDtypeStruct(s.shape, s.dtype) for s in state],
            input_output_aliases={6: 1, 7: 2, 8: 3},
            compiler_params=pltpu.CompilerParams(vmem_limit_bytes=24 * MEBI),
            cost_estimate=cost,
            name="forward_block",
        )(flags, entries, incoming, norm_gain, weights, input_map, *state)
        return following, state

    def backward(flags, incoming, state, grads):
        return pl.pallas_call(
            backward_kernel,
            grid_spec=pltpu.PrefetchScalarGridSpec(
                num_scalar_prefetch=1,
                grid=(1,),
                in_specs=[
                    entering(), whole(), slotted((rows, width)), slotted((rows, inner)),
                    slotted((rows, features)), whole(), whole(), whole(), untouched,
                ],
                out_specs=[whole(), slotted((signals, features))],
                scratch_shapes=[pltpu.VMEM((rows, width), f32), pltpu.VMEM((rows, inner), bf16)],
            ),
            out_shape=[
                jax.ShapeDtypeStruct((rows, width), bf16),
                jax.ShapeDtypeStruct(grads.shape, grads.dtype),
            ],
            input_output_aliases={9: 1},
            compiler_params=pltpu.CompilerParams(vmem_limit_bytes=24 * MEBI),
            cost_estimate=cost,
            name="backward_block",
        )(flags, targets, incoming, *state, norm_gain, weights, output_map, grads)

    slots = batches + 1
    state = (
        jnp.zeros((slots, rows, width), bf16),
        jnp.zeros((slots, rows, inner), f32),
        jnp.zeros((slots, rows, features), bf16),
    )
    grads = jnp.zeros((slots, signals, features), f32)
    up = jnp.zeros((rows, width), bf16)
    down = jnp.zeros((rows, width), bf16)
    for tick in range(2 * sections + batches - 1):
        stages = [tick - m for m in range(batches)]
        back = [s for s in stages if sections <= s < 2 * sections]
        ahead = [s for s in stages if 0 <= s < sections]
        if back:
            down, grads = backward(flags_at(tick - (2 * sections - 1 - section)), down, state, grads)
            pairs = [(2 * sections - 1 - s, 2 * sections - 2 - s) for s in back if s < 2 * sections - 1]
            if pairs:
                down = lax.ppermute(down, "section", pairs)
        if ahead:
            up, state = forward(flags_at(tick - section), up, state)
            pairs = [(s, s + 1) for s in ahead if s < sections - 1]
            if pairs:
                up = lax.ppermute(up, "section", pairs)

    flat = grads[:batches].reshape(batches, signals * features)
    everyone = lax.all_to_all(
        jnp.broadcast_to(flat[None], (lax.axis_size("dp"), *flat.shape)), "dp", 0, 0, tiled=True
    ).reshape(-1, flat.shape[1])
    owners = jnp.arange(everyone.shape[0], dtype=jnp.int32)
    select = (owners[:, None] == query_examples[None, :]).astype(f32)
    mine = lax.axis_index("dp") * batches + jnp.arange(batches, dtype=jnp.int32)
    own = (mine[:, None] == owners[None, :]).astype(f32)
    section_scores = pl.pallas_call(
        scores_kernel,
        out_shape=jax.ShapeDtypeStruct((batches, select.shape[1]), f32),
        in_specs=[whole()] * 4,
        out_specs=whole(),
        compiler_params=pltpu.CompilerParams(vmem_limit_bytes=24 * MEBI),
        name="section_scores",
    )(everyone, own, inverse, select)
    shares = lax.all_to_all(
        jnp.broadcast_to(section_scores[None], (sections, *section_scores.shape)),
        "section", 0, 0, tiled=True,
    )
    return shares.sum(axis=0)


def solution(mesh):
    placed = (
        P("dp", None),
        P("dp", None),
        P("dp"),
        P(),
        P("section", None),
        P("section", "dp", None),
        P("section", "dp", None),
        P("section", None, None),
        P("section", None, None),
        P("section", None, None),
    )
    return jax.shard_map(
        per_device, mesh=mesh, in_specs=placed, out_specs=P("dp", None), check_vma=False
    )
```

time: 938 us -> 764 us (0.81)
  other arithmetic: 288 us -> 5.27 us
  Pallas kernels: 0 us -> 211 us
  local copies, waits for them, and re-layouts: 73.4 us -> 194 us
  matrix products: 87.2 us -> 0 us
  waiting for transfers between devices: 374 us -> 289 us
  starting transfers between devices: 78.8 us -> 33.3 us
    another operation x33 -> x0, other arithmetic: 256 us -> none  [the longest x30 172 us: per_device(): lower_factor = jnp.linalg.cholesky(hessian)]
    pallas_call x0 -> x20, Pallas kernels: none -> 211 us  [the longest x1 122 us: minus_inverse(): pl.pallas_call(inverse_kernel, out_shape=jax.ShapeDtypeStruct(prior.shape...]
    unnamed x25 -> x254, local copies, waits for them, and re-layouts: 7.51 us -> 181 us
    ppermute x18 -> x16, waiting for transfers between devices: 228 us -> 135 us  [the longest x8 112 us: per_device(): down = lax.ppermute(down, 'section', pairs)]
    another operation x44 -> x0, matrix products: 43.6 us -> none  [the longest x14 23.1 us: per_device(): lower_factor = jnp.linalg.cholesky(hessian)]
    dot_general x15 -> x0, matrix products: 43.5 us -> none  [the longest x2 11.6 us: forward_block(): values = jnp.dot(normed, value_map, preferred_element_type=jnp.float32)]
    ppermute x18 -> x16, starting transfers between devices: 63 us -> 27.9 us  [the longest x8 15.5 us: per_device(): up = lax.ppermute(up, 'section', pairs)]
    another operation x53 -> x19, local copies, waits for them, and re-layouts: 32.5 us -> 11.1 us  [the longest x18 11.1 us: flags_at(): jnp.stack([active.astype(jnp.int32), first, last, slot, entry])]
  transfers between devices with their start and end apart: 20 -> 18, of which waited for: 20 -> 7; matrix products, arithmetic and copies ran while one was open for 1% -> 2% of each run, Pallas kernels for 0% -> 17%
where the time goes in v1:
time: 764 us; the launch traced here: 753 us
  waiting for transfers between devices  289 us (38%)
  Pallas kernels  211 us (28%)
  local copies, waits for them, and re-layouts  194 us (25%)
  starting transfers between devices  33.3 us (4%)
  between operations  14.1 us (2%)
    unnamed x254, local copies, waits for them, and re-layouts  181 us
    all_gather x1, waiting for transfers between devices, per_device(): weights = lax.all_gather(both, 'dp', axis=1, tiled=True)  145 us
    pallas_call x1, Pallas kernels, minus_inverse(): pl.pallas_call(inverse_kernel, out_shape=jax.ShapeDtypeStruct(prior.shape...  122 us
    ppermute x8, waiting for transfers between devices, per_device(): down = lax.ppermute(down, 'section', pairs)  112 us
    pallas_call x9, Pallas kernels, backward(): pl.pallas_call(backward_kernel, grid_spec=pltpu.PrefetchScalarGridSpec(nu...  40.4 us
    pallas_call x9, Pallas kernels, forward(): pl.pallas_call(forward_kernel, grid_spec=pltpu.PrefetchScalarGridSpec(num...  39.8 us
    ppermute x8, waiting for transfers between devices, per_device(): up = lax.ppermute(up, 'section', pairs)  23.6 us
    ppermute x8, starting transfers between devices, per_device(): up = lax.ppermute(up, 'section', pairs)  15.5 us
  transfers between devices with their start and end apart: 18, of which 7 were waited for; matrix products, arithmetic and copies ran while one was open for 2% of the time, Pallas kernels for 17%

profile of v1, /device:TPU:1, one launch (start us, length us, event | category | flops | bytes accessed | tf_op | source)
XLA Modules:
  0.0 753.0 jit_solution(507537258827742634)
XLA Ops:
  6.5 1.9 pad_maximum_fusion
  9.1 144.9 %all-gather.2.cloned.1.call-done.weights = bf16[2,4096,1024]{2,1,0:T(8,128)(2,1)} async-done(((bf16[2,128,1024]{2,1,0:T(8,128)(2,1)}), bf16[2,4096,1024]{2,1,0:T(8,128)(2,1)}) %all-gather.2.cloned.1.call-update) | async-done | bytes 16777232 | tf_op jit(solution)/shard_map/all_gather | solution.py:186
  155.7 5.8 copy-done
  161.5 1.4 forward_block.9
  165.5 7.4 collective-permute-done.incoming
  172.9 5.8 copy-done.1
  182.6 7.4 forward_block.10
  190.6 1.9 collective-permute-start.1
  193.2 8.6 %collective-permute-done.1.incoming = bf16[96,4096]{1,0:T(8,128)(2,1)} collective-permute-done((bf16[96,4096]{1,0:T(8,128)(2,1)}, bf16[96,4096]{1,0:T(8,128)(2,1)}, u32[]{:S(2)}, u32[]{:S(2)}) %collective-permute-start.1) | collective-permute-done | bytes 786464 | tf_op jit(solution)/shard_map/ppermute | solution.py:285
  201.8 5.8 copy-done.2
  211.4 7.4 forward_block.11
  219.5 5.3 collective-permute-start.2
  225.4 7.7 %collective-permute-done.2.incoming = bf16[96,4096]{1,0:T(8,128)(2,1)} collective-permute-done((bf16[96,4096]{1,0:T(8,128)(2,1)}, bf16[96,4096]{1,0:T(8,128)(2,1)}, u32[]{:S(2)}, u32[]{:S(2)}) %collective-permute-start.2) | collective-permute-done | bytes 786464 | tf_op jit(solution)/shard_map/ppermute | solution.py:285
  233.1 5.8 copy-done.3
  242.7 12.2 %forward_block.12 = (bf16[96,4096]{1,0:T(8,128)(2,1)}, bf16[3,96,4096]{2,1,0:T(8,128)(2,1)S(1)}, f32[3,96,1024]{2,1,0:T(8,128)S(1)}, bf16[3,96,32]{2,1,0:T(8,128)(2,1)S(1)}) custom-call(s32[5]{0:T(128)S(1)} %copy-done.118, bf16[2,96,4096]{2,1,0:T(8,128)(2,1)S(1)} %bitcast.66, ...), custom_call_target="tpu_custom_call", output_to_operand_aliasing={{1}: (6, {}), {2}: (7, {}), {3}: (8, {})} | custom-call | flops 1610612736 | bytes 16777216 | tf_op jit(solution)/shard_map/forward_block/pallas_call | solution.py:222
  255.6 1.5 collective-permute-start.3
  257.8 5.8 copy-done.4
  267.5 2.6 forward_block.13
  270.7 1.5 collective-permute-start.4
  272.9 5.8 copy-done.5
  282.5 2.6 forward_block.14
  285.7 1.5 collective-permute-start.5
  289.8 5.8 copy-done.6
  299.4 1.9 forward_block.15
  303.6 2.5 copy-done.17
  306.9 1.7 forward_block.16
  310.0 1.6 collective-permute-start.8
  311.7 1.7 copy-done.19
  315.9 1.4 backward_block.9
  319.4 5.8 copy-done.7
  325.2 1.7 copy-done.20
  329.2 2.6 forward_block.17
  334.8 5.8 copy-done.8
  340.5 1.7 copy-done.22
  344.2 1.5 backward_block.10
  346.3 1.5 collective-permute-start.9
  348.5 5.8 copy-done.9
  358.9 10.9 %backward_block.11 = (bf16[96,4096]{1,0:T(8,128)(2,1)}, f32[3,32,32]{2,1,0:T(8,128)S(1)}) custom-call(s32[5]{0:T(128)S(1)} %copy-done.107, bf16[2,96,4096]{2,1,0:T(8,128)(2,1)S(1)} %copy-done.26, bf16[96,4096]{1,0:T(8,128)(2,1)} %collective-permute-done.9.incoming, bf16[3,96,4096]{2,1,0:T(8,128)(2,1)S(1)} %copy-done.23, ...), custom_call_target="tpu_custom_call", output_to_operand_aliasing={{1}: (9, {})} | custom-call | flops 1610612736 | bytes 16777216 | tf_op jit(solution)/shard_map/backward_block/pallas_call | solution.py:241
  370.4 1.5 collective-permute-start.10
  372.6 5.8 copy-done.10
  383.0 2.6 backward_block.12
  386.1 1.5 collective-permute-start.11
  388.3 5.8 copy-done.11
  398.7 2.6 backward_block.13
  401.9 1.5 collective-permute-start.12
  404.1 5.8 copy-done.12
  414.5 2.6 backward_block.14
  419.6 100.8 %collective-permute-done.13.incoming = bf16[96,4096]{1,0:T(8,128)(2,1)} collective-permute-done((bf16[96,4096]{1,0:T(8,128)(2,1)}, bf16[96,4096]{1,0:T(8,128)(2,1)}, u32[]{:S(2)}, u32[]{:S(2)}) %collective-permute-start.13) | collective-permute-done | bytes 786464 | tf_op jit(solution)/shard_map/ppermute | solution.py:280
  520.4 5.8 copy-done.13
  530.8 8.3 %backward_block.15 = (bf16[96,4096]{1,0:T(8,128)(2,1)}, f32[3,32,32]{2,1,0:T(8,128)S(1)}) custom-call(s32[5]{0:T(128)S(1)} %copy-done.111, bf16[2,96,4096]{2,1,0:T(8,128)(2,1)S(1)} %copy-done.30, bf16[96,4096]{1,0:T(8,128)(2,1)} %collective-permute-done.13.incoming, bf16[3,96,4096]{2,1,0:T(8,128)(2,1)S(1)} %copy-done.23, ...), custom_call_target="tpu_custom_call", output_to_operand_aliasing={{1}: (9, {})} | custom-call | flops 1610612736 | bytes 16777216 | tf_op jit(solution)/shard_map/backward_block/pallas_call | solution.py:241
  539.7 1.9 collective-permute-start.14
  542.3 11.0 %collective-permute-done.14.incoming = bf16[96,4096]{1,0:T(8,128)(2,1)} collective-permute-done((bf16[96,4096]{1,0:T(8,128)(2,1)}, bf16[96,4096]{1,0:T(8,128)(2,1)}, u32[]{:S(2)}, u32[]{:S(2)}) %collective-permute-start.14) | collective-permute-done | bytes 786464 | tf_op jit(solution)/shard_map/ppermute | solution.py:280
  553.4 5.8 copy-done.14
  563.7 7.8 %backward_block.16 = (bf16[96,4096]{1,0:T(8,128)(2,1)}, f32[3,32,32]{2,1,0:T(8,128)S(1)}) custom-call(s32[5]{0:T(128)S(1)} %copy-done.112, bf16[2,96,4096]{2,1,0:T(8,128)(2,1)S(1)} %copy-done.31, bf16[96,4096]{1,0:T(8,128)(2,1)} %collective-permute-done.14.incoming, bf16[3,96,4096]{2,1,0:T(8,128)(2,1)S(1)} %copy-done.23, ...), custom_call_target="tpu_custom_call", output_to_operand_aliasing={{1}: (9, {})} | custom-call | flops 1610612736 | bytes 16777216 | tf_op jit(solution)/shard_map/backward_block/pallas_call | solution.py:241
  572.2 2.4 collective-permute-start.15
  574.6 122.2 %prior_inverse.1.inverse = f32[1024,1024]{1,0:T(8,128)S(1)} custom-call(f32[1024,1024]{1,0:T(8,128)S(1)} %bitcast.90), custom_call_target="tpu_custom_call" | custom-call | flops 64424509440 | bytes 8388608 | tf_op jit(solution)/shard_map/prior_inverse/pallas_call | solution.py:65
  696.8 2.0 copy-done.100
  699.4 5.8 copy-done.15
  709.7 2.7 backward_block.17
  713.3 5.4 all-to-all-start
  719.4 8.9 %all-to-all-done = f32[32,2,1024]{2,1,0:T(2,128)S(1)} async-done(((f32[32,2,1024]{2,1,0:T(2,128)}), f32[32,2,1024]{2,1,0:T(2,128)S(1)}, u32[]{:S(2)}, u32[]{:S(2)}) %all-to-all-start) | async-done | bytes 262176 | tf_op jit(solution)/shard_map/all_to_all | solution.py:288
  728.5 2.2 copy-done.101
  730.7 8.4 %section_scores.1 = f32[2,16]{1,0:T(2,128)S(1)} custom-call(f32[64,1024]{1,0:T(8,128)S(1)} %reshape.40.every, f32[2,64]{1,0:T(2,128)S(1)} %compare_convert_fusion.own, f32[1024,1024]{1,0:T(8,128)S(1)} %copy-done.101, f32[64,16]{1,0:T(8,128)S(1)} %fusion.select), custom_call_target="tpu_custom_call" | custom-call | tf_op jit(solution)/shard_map/section_scores/pallas_call | solution.py:295
  739.1 6.2 all_to_all.10
  (284 shorter events, 97.6 us)
Async XLA Ops:
  6.5 147.4 %all-gather.2.cloned.1.call-start = ((), (), s32[]{:S(2)}) async-start(), calls=%async_computation.2 | async-start | bytes 17301504 | tf_op jit(solution)/shard_map/all_gather | solution.py:186
  154.0 1.7 copy-start.33
  154.0 1.7 copy-start.64
  154.0 1.7 copy-start.99
  154.1 1.7 copy-start.115
  155.7 5.8 copy-start
  163.6 9.4 %collective-permute-start = (bf16[96,4096]{1,0:T(8,128)(2,1)}, bf16[96,4096]{1,0:T(8,128)(2,1)}, u32[]{:S(2)}, u32[]{:S(2)}) collective-permute-start(bf16[96,4096]{1,0:T(8,128)(2,1)} %get-tuple-element.57), channel_id=1, source_target_pairs={{0,32},{1,33},{2,34},{3,35},{4,36},{5,37},{6,38},{7,39},{8,40},{9,... | collective-permute-start | bytes 2359304 | tf_op jit(solution)/shard_map/ppermute | solution.py:285
  172.9 5.8 copy-start.1
  178.7 1.4 copy-start.34
  190.6 11.1 %collective-permute-start.1 = (bf16[96,4096]{1,0:T(8,128)(2,1)}, bf16[96,4096]{1,0:T(8,128)(2,1)}, u32[]{:S(2)}, u32[]{:S(2)}) collective-permute-start(bf16[96,4096]{1,0:T(8,128)(2,1)} %get-tuple-element.61), channel_id=1, source_target_pairs={{32,64},{0,32},{33,65},{1,33},{34,66},{2,34},{35,67},{3,35},{36,68... | collective-permute-start | bytes 2359304 | tf_op jit(solution)/shard_map/ppermute | solution.py:285
  201.8 5.8 copy-start.2
  207.5 1.4 copy-start.35
  219.5 13.6 %collective-permute-start.2 = (bf16[96,4096]{1,0:T(8,128)(2,1)}, bf16[96,4096]{1,0:T(8,128)(2,1)}, u32[]{:S(2)}, u32[]{:S(2)}) collective-permute-start(bf16[96,4096]{1,0:T(8,128)(2,1)} %get-tuple-element.65), channel_id=1, source_target_pairs={{64,96},{32,64},{65,97},{33,65},{66,98},{34,66},{67,99},{35,67},{6... | collective-permute-start | bytes 2359304 | tf_op jit(solution)/shard_map/ppermute | solution.py:285
  233.1 5.8 copy-start.3
  255.6 2.2 collective-permute-start.3
  257.8 5.8 copy-start.4
  270.7 2.2 collective-permute-start.4
  272.9 5.8 copy-start.5
  285.7 4.1 collective-permute-start.5
  289.8 5.8 copy-start.6
  299.4 2.8 copy-start.122
  299.4 4.2 copy-start.113
  299.4 12.2 %slice-start = ((s8[16777216]{0:T(1024)(128)(4,1)}), s8[4194304]{0:T(1024)(128)(4,1)S(1)}, s32[]{:S(2)}) async-start(s8[16777216]{0:T(1024)(128)(4,1)} %bitcast.61), calls=%async_computation.3 | async-start | bytes 8388608
  299.4 12.2 %slice-start.1 = ((s8[16777216]{0:T(1024)(128)(4,1)}), s8[4194304]{0:T(1024)(128)(4,1)S(1)}, s32[]{:S(2)}) async-start(s8[16777216]{0:T(1024)(128)(4,1)} %bitcast.61), calls=%async_computation.4 | async-start | bytes 8388608
  301.4 2.2 copy-start.16
  301.4 2.2 copy-start.53
  301.4 2.2 collective-permute-start.6
  302.2 9.4 %slice-start.2 = ((s8[16777216]{0:T(1024)(128)(4,1)}), s8[4194304]{0:T(1024)(128)(4,1)S(1)}, s32[]{:S(2)}) async-start(s8[16777216]{0:T(1024)(128)(4,1)} %bitcast.61), calls=%async_computation.5 | async-start | bytes 8388608
  303.6 2.5 copy-start.17
  306.9 4.7 slice-start.3
  306.9 4.7 copy-start.90
  306.9 4.7 copy-start.104
  308.6 1.4 copy-start.18
  310.0 9.4 %collective-permute-start.8 = (bf16[96,4096]{1,0:T(8,128)(2,1)}, bf16[96,4096]{1,0:T(8,128)(2,1)}, u32[]{:S(2)}, u32[]{:S(2)}) collective-permute-start(bf16[96,4096]{1,0:T(8,128)(2,1)} %get-tuple-element.89), channel_id=1, source_target_pairs={{192,224},{193,225},{194,226},{195,227},{196,228},{197,229},{198,2... | collective-permute-start | bytes 2359304 | tf_op jit(solution)/shard_map/ppermute | solution.py:285
  311.6 1.7 copy-start.19
  317.9 15.9 %collective-permute-start.7 = (bf16[96,4096]{1,0:T(8,128)(2,1)}, bf16[96,4096]{1,0:T(8,128)(2,1)S(1)}, u32[]{:S(2)}, u32[]{:S(2)}) collective-permute-start(bf16[96,4096]{1,0:T(8,128)(2,1)} %get-tuple-element.88), channel_id=1, source_target_pairs={{224,192},{225,193},{226,194},{227,195},{228,196},{229,197},{230,1... | collective-permute-start | bytes 2359304 | tf_op jit(solution)/shard_map/ppermute | solution.py:280
  319.4 5.8 copy-start.7
  325.2 1.7 copy-start.20
  329.2 5.5 copy-start.25
  329.2 5.5 copy-start.75
  329.2 5.5 copy-start.91
  329.2 5.5 copy-start.105
  331.8 1.4 copy-start.21
  334.7 5.8 copy-start.8
  340.5 1.7 copy-start.22
  344.2 4.3 copy-start.23
  346.3 2.2 collective-permute-start.9
  348.5 5.8 copy-start.9
  370.4 2.2 collective-permute-start.10
  372.6 5.8 copy-start.10
  386.1 2.2 collective-permute-start.11
  388.3 5.8 copy-start.11
  401.9 2.2 collective-permute-start.12
  404.1 5.8 copy-start.12
  417.6 102.8 %collective-permute-start.13 = (bf16[96,4096]{1,0:T(8,128)(2,1)}, bf16[96,4096]{1,0:T(8,128)(2,1)}, u32[]{:S(2)}, u32[]{:S(2)}) collective-permute-start(bf16[96,4096]{1,0:T(8,128)(2,1)} %get-tuple-element.102), channel_id=1, source_target_pairs={{64,32},{96,64},{65,33},{97,65},{66,34},{98,66},{67,35},{99,67},{6... | collective-permute-start | bytes 2359304 | tf_op jit(solution)/shard_map/ppermute | solution.py:280
  520.4 5.8 copy-start.13
  539.7 13.6 %collective-permute-start.14 = (bf16[96,4096]{1,0:T(8,128)(2,1)}, bf16[96,4096]{1,0:T(8,128)(2,1)}, u32[]{:S(2)}, u32[]{:S(2)}) collective-permute-start(bf16[96,4096]{1,0:T(8,128)(2,1)} %get-tuple-element.104), channel_id=1, source_target_pairs={{32,0},{64,32},{33,1},{65,33},{34,2},{66,34},{35,3},{67,35},{36,4}... | collective-permute-start | bytes 2359304 | tf_op jit(solution)/shard_map/ppermute | solution.py:280
  553.4 5.8 copy-start.14
  563.7 10.8 %copy-start.121 = (f32[1,1024,1024]{2,1,0:T(8,128)S(1)}, f32[1,1024,1024]{2,1,0:T(8,128)}, u32[]{:S(2)}) copy-start(f32[1,1024,1024]{2,1,0:T(8,128)} %param.19) | copy-start | bytes 12582916
  572.2 127.2 %collective-permute-start.15 = (bf16[96,4096]{1,0:T(8,128)(2,1)}, bf16[96,4096]{1,0:T(8,128)(2,1)}, u32[]{:S(2)}, u32[]{:S(2)}) collective-permute-start(bf16[96,4096]{1,0:T(8,128)(2,1)} %get-tuple-element.106), channel_id=1, source_target_pairs={{32,0},{33,1},{34,2},{35,3},{36,4},{37,5},{38,6},{39,7},{40,8},{41... | collective-permute-start | bytes 2359304 | tf_op jit(solution)/shard_map/ppermute | solution.py:280
  696.8 2.0 copy-start.100
  699.4 5.8 copy-start.15
  713.3 15.0 %all-to-all-start = ((f32[32,2,1024]{2,1,0:T(2,128)}), f32[32,2,1024]{2,1,0:T(2,128)S(1)}, u32[]{:S(2)}, u32[]{:S(2)}) async-start(f32[32,2,1024]{2,1,0:T(2,128)} %broadcast_in_dim.37), calls=%async_computation | async-start | bytes 524288 | tf_op jit(solution)/shard_map/all_to_all | solution.py:288
  728.5 2.2 copy-start.101
  (81 other events, 71.4 us)
Sparse Core Ops, SparseCore 0:
  9.9 143.9 all-gather.1
